TPU v7x, 256 devices: a whole 4x4x8 slice. The times are simulated.
256 devices in a mesh: gx: 4 (over y), gy: 8 (over x, core), gz: 8 (over z).
Axes of the slice: x: 4, y: 4, z: 8, core: 2. Of those that a mesh axis runs over, the one named last changes fastest.
Arguments:
- basis: bfloat16 [8, 3, 64, 1024, 128], P('gx', None, 'gy', 'gz'), may hold values from -4.8 to 4.8
- modal_now: bfloat16 [128, 8], replicated, may hold values from -0.5 to 0.5
- modal_prev: bfloat16 [128, 8], replicated, may hold values from -0.5 to 0.5
- material_ids: int32 [8, 64, 1024], P('gx', 'gy', 'gz'), may hold values from 0 to 3
- moduli: float32 [3, 4], replicated, may hold values from 0.4 to 1.6
- drive_mask: int32 [8, 8, 64, 1024], P(None, 'gx', 'gy', 'gz'), may hold values 0 or 1
- drive: float32 [3, 8], replicated, may hold values from -8 to 8
Outputs:
- displacement: float32 [3, 8, 8, 64, 1024], P(None, None, 'gx', 'gy', 'gz')
- modes: float32 [3, 8, 8, 64, 1024], P(None, None, 'gx', 'gy', 'gz')
- coefficients: float32 [4, 2, 128, 8], replicated
- rfactor: float32 [4, 8, 8], replicated
All inputs are finite; a program needn't handle non-finite values. No bound on the sum of `drive_mask` on one device may be relied on, other than what follows from the above.
Results may differ from a plain program's by a relative error of at most 0.0008.
The roundings to bfloat16 on the way count: a program that leaves them out, or rounds other values in their place, can miss the bound.
Values sent between devices are 32-bit elements; how exact they have to be, the bound alone decides.
No kernel may reach another device: no remote copies, remote signals or barrier semaphores. Data moves between devices by JAX's collectives and lax.ppermute only.
A program may use at most 128 MiB of HBM per device.

v0:
```python
import jax
import jax.numpy as jnp
from jax import lax
from jax.sharding import PartitionSpec as P

STEPS = 4
step_squared = 0.1
ramp_steps = 4.0


def padded_2(block, sides, width):
    for axis, dim in sides:
        count = lax.axis_size(axis)
        forward = [(i, i + 1) for i in range(count - 1)]
        backward = [(target, source) for source, target in forward]
        low = lax.ppermute(
            lax.slice_in_dim(block, block.shape[dim] - width, None, axis=dim), axis, forward
        )
        high = lax.ppermute(lax.slice_in_dim(block, 0, width, axis=dim), axis, backward)
        block = jnp.concatenate([low, block, high], axis=dim)
    return block


def interior(array, direction_axis, offset):
    base_axis = array.ndim - 3
    result = array
    for axis_index in range(3):
        extent = array.shape[base_axis + axis_index]
        begin = offset if axis_index == direction_axis else 1
        result = lax.slice_in_dim(result, begin, extent - 2 + begin, axis=base_axis + axis_index)
    return result


def stiffness(field, material_props):
    component_rows = []
    for component in range(3):
        center = interior(field[component], 0, 1)
        accumulated = jnp.zeros_like(center)
        for direction_axis in range(3):
            modulus = material_props[0] if component == direction_axis else material_props[1]
            center_modulus = interior(modulus, 0, 1)
            for offset in (0, 2):
                coupling = 0.5 * (center_modulus + interior(modulus, direction_axis, offset))
                accumulated = accumulated + coupling * (
                    center - interior(field[component], direction_axis, offset)
                )
        component_rows.append(accumulated)
    return jnp.stack(component_rows)


def lookup(material_ids, moduli):
    levels = jnp.arange(moduli.shape[1], dtype=jnp.int32)
    onehot = (material_ids[None] == levels[:, None, None, None]).astype(jnp.float32)
    return jnp.einsum("mxyz,pm->pxyz", onehot, moduli, precision=lax.Precision.HIGHEST)


def expand(basis, coefficient):
    return jnp.einsum("xcyzk,kj->cjxyz", basis, coefficient, preferred_element_type=jnp.float32)


def project(basis, field):
    return jnp.einsum("xcyzk,cjxyz->kj", basis, field, preferred_element_type=jnp.float32)


def apply_inverse(block, lower_factor):
    identity_block = jnp.eye(lower_factor.shape[0], dtype=jnp.float32)
    lower_inverse = jax.scipy.linalg.solve_triangular(lower_factor, identity_block, lower=True)
    return jnp.einsum("cixyz,ji->cjxyz", block, lower_inverse, precision=lax.Precision.HIGHEST)


def local_gram(block):
    return jnp.einsum("cixyz,cjxyz->ij", block, block, precision=lax.Precision.HIGHEST)


def orthonormalize(following, basis, dof_weight):
    highest = lax.Precision.HIGHEST
    snapshot = following.astype(jnp.bfloat16)
    partial_coef = project(basis, snapshot) * dof_weight
    first_coef = lax.psum(partial_coef, ("gx", "gy", "gz"))
    first_resid = snapshot.astype(jnp.float32) - expand(basis, first_coef.astype(jnp.bfloat16))
    first_gram = lax.psum(local_gram(first_resid) * dof_weight, ("gx", "gy", "gz"))
    first_lower = jnp.linalg.cholesky(first_gram)
    first_q = apply_inverse(first_resid, first_lower)
    second_coef = lax.psum(
        project(basis, first_q.astype(jnp.bfloat16)) * dof_weight, ("gx", "gy", "gz")
    )
    second_resid = first_q - expand(basis, second_coef.astype(jnp.bfloat16))
    second_gram = lax.psum(local_gram(second_resid) * dof_weight, ("gx", "gy", "gz"))
    second_lower = jnp.linalg.cholesky(second_gram)
    modes = apply_inverse(second_resid, second_lower)
    factor = jnp.dot(first_lower, second_lower, precision=highest).T
    return (jnp.stack([first_coef, second_coef]), factor, modes)


def shards(basis, modal_now, modal_prev, material_ids, moduli, drive_mask, drive):
    devices_total = lax.axis_size("gx") * lax.axis_size("gy") * lax.axis_size("gz")
    dof_weight = 1.0 / (3.0 * basis.shape[0] * basis.shape[2] * basis.shape[3] * devices_total)
    current = expand(basis, modal_now)
    earlier = expand(basis, modal_prev)
    material_props = lookup(material_ids, moduli)
    port_mask = drive_mask.astype(jnp.float32)
    static = jnp.concatenate([material_props, port_mask], axis=0)
    wide_static = padded_2(static, (("gx", 1), ("gy", 2), ("gz", 3)), 2)
    props_wide = wide_static[:3]
    props_near = props_wide[:, 1:-1, 1:-1, 1:-1]
    inverse_mass = material_props[2]
    drive_field = drive[:, :, None, None, None]
    coefficient_list = []
    factor_list = []
    modes = current
    for step in range(STEPS):
        padded = padded_2(current, (("gx", 2), ("gy", 3), ("gz", 4)), 1)
        ramp_level = min(1.0, (step + 1) / ramp_steps)
        load_field = drive_field * port_mask[None] * ramp_level
        following = (
            2.0 * current
            - earlier
            + step_squared * inverse_mass * (load_field - stiffness(padded, props_near))
        )
        earlier = current
        current = following
        coefs, factor, modes = orthonormalize(following, basis, dof_weight)
        coefficient_list.append(coefs)
        factor_list.append(factor)
    return (current, modes, jnp.stack(coefficient_list), jnp.stack(factor_list))


def solution(mesh):
    in_specs = (
        P("gx", None, "gy", "gz", None),
        P(),
        P(),
        P("gx", "gy", "gz"),
        P(),
        P(None, "gx", "gy", "gz"),
        P(),
    )
    out_specs = (P(None, None, "gx", "gy", "gz"), P(None, None, "gx", "gy", "gz"), P(), P())
    return jax.shard_map(shards, mesh=mesh, in_specs=in_specs, out_specs=out_specs, check_vma=False)
```

profile of v0, /device:TPU:1, one launch (start us, length us, event | category | flops | bytes accessed | tf_op | source)
XLA Modules:
  0.0 537.8 jit_solution(7000948003984317785)
XLA Ops:
  2.5 4.0 collective-permute-start
  9.1 4.0 collective-permute-start.6
  14.7 3.7 collective-permute-done.7
  18.5 5.7 %collective-permute-start.8 = (f32[3,8,4,1,128]{4,1,3,2,0:T(8,128)S(1)}, f32[3,8,4,1,128]{4,1,3,2,0:T(8,128)S(1)}, u32[]{:S(2)}, u32[]{:S(2)}) collective-permute-start(f32[3,8,4,1,128]{4,1,3,2,0:T(8,128)S(1)} %get-tuple-element.78), channel_id=1, source_target_pairs={{0,8},{8,16},{16,24},{24,32},{32,40},{40,48},{48,56},{1,9},{9,17},... | collective-permute-start | bytes 147464 | tf_op jit(solution)/shard_map/ppermute | solution.py:16
  30.7 3.6 collective-permute-start.10
  35.7 3.8 copy.222
  49.6 4.5 copy.221
  54.1 3.9 copy.223
  58.0 9.0 %pad_maximum_fusion = f32[11,6,12,128]{2,1,3,0:T(8,128)S(1)} fusion(f32[11,6,2,128]{2,1,3,0:T(8,128)} %copy.223, f32[11,6,8,128]{2,1,3,0:T(8,128)} %copy.222, f32[11,6,2,128]{2,1,3,0:T(8,128)} %copy.221), kind=kLoop, calls=%fused_computation | loop fusion | flops 202752 | bytes 811008 | tf_op jit(solution)/shard_map/concatenate | solution.py:20
  69.5 3.5 collective-permute-start.4
  75.3 4.2 copy.225
  91.7 3.9 collective-permute-done.13
  95.6 5.9 %collective-permute-start.14 = (f32[3,8,4,1,128]{4,1,3,2,0:T(8,128)S(1)}, f32[3,8,4,1,128]{4,1,3,2,0:T(8,128)S(1)}, u32[]{:S(2)}, u32[]{:S(2)}) collective-permute-start(f32[3,8,4,1,128]{4,1,3,2,0:T(8,128)S(1)} %get-tuple-element.76), channel_id=1, source_target_pairs={{0,8},{8,16},{16,24},{24,32},{32,40},{40,48},{48,56},{1,9},{9,17},... | collective-permute-start | bytes 147464 | tf_op jit(solution)/shard_map/ppermute | solution.py:16
  103.5 3.5 collective-permute-done.15
  107.2 4.9 collective-permute-start.16
  113.4 7.9 %collective-permute-done.16 = f32[3,8,4,10,1]{4,1,3,2,0:T(8,128)S(1)} collective-permute-done((f32[3,8,4,10,1]{4,1,3,2,0:T(8,128)S(1)}, f32[3,8,4,10,1]{4,1,3,2,0:T(8,128)S(1)}, u32[]{:S(2)}, u32[]{:S(2)}) %collective-permute-start.16) | collective-permute-done | bytes 3872 | tf_op jit(solution)/shard_map/ppermute | solution.py:16
  121.3 5.2 collective-permute-done.17
  132.5 4.1 collective-permute-done.19
  136.7 5.3 collective-permute-start.20
  143.9 3.5 collective-permute-done.21
  147.6 3.7 collective-permute-start.22
  152.8 7.7 %collective-permute-done.22 = f32[3,8,4,10,1]{4,1,3,2,0:T(8,128)S(1)} collective-permute-done((f32[3,8,4,10,1]{4,1,3,2,0:T(8,128)S(1)}, f32[3,8,4,10,1]{4,1,3,2,0:T(8,128)S(1)}, u32[]{:S(2)}, u32[]{:S(2)}) %collective-permute-start.22) | collective-permute-done | bytes 3872 | tf_op jit(solution)/shard_map/ppermute | solution.py:16
  160.5 4.1 collective-permute-done.23
  169.6 4.1 collective-permute-done.25
  173.7 4.8 collective-permute-start.26
  184.2 4.6 collective-permute-start.28
  190.4 7.6 %collective-permute-done.28 = f32[3,8,4,10,1]{4,1,3,2,0:T(8,128)S(1)} collective-permute-done((f32[3,8,4,10,1]{4,1,3,2,0:T(8,128)S(1)}, f32[3,8,4,10,1]{4,1,3,2,0:T(8,128)S(1)}, u32[]{:S(2)}, u32[]{:S(2)}) %collective-permute-start.28) | collective-permute-done | bytes 3872 | tf_op jit(solution)/shard_map/ppermute | solution.py:16
  198.0 4.1 collective-permute-done.29
  203.5 73.7 %all-reduce.3 = (f32[128,8]{0,1:T(8,128)S(1)}, f32[128,8]{0,1:T(8,128)S(1)}, f32[128,8]{0,1:T(8,128)S(1)}, f32[128,8]{0,1:T(8,128)S(1)}) all-reduce(f32[128,8]{0,1:T(8,128)S(1)} %fusion.25, f32[128,8]{0,1:T(8,128)S(1)} %fusion.13, f32[128,8]{0,1:T(8,128)S(1)} %fusion.17, ...), channel_id=1, replica_groups=mesh['gx'=4,'gy'=8,'gz'=8] {'gx','gy','gz'}, use_global_device_ids=true, to_apply=%region_0.0 | all-reduce | flops 4096 | bytes 32768 | tf_op jit(solution)/shard_map/psum | solution.py:79
  281.4 73.0 %all-reduce.2 = (f32[8,8]{0,1:T(8,128)S(1)}, f32[8,8]{0,1:T(8,128)S(1)}, f32[8,8]{0,1:T(8,128)S(1)}, f32[8,8]{0,1:T(8,128)S(1)}) all-reduce(f32[8,8]{0,1:T(8,128)S(1)} %fusion.33, f32[8,8]{0,1:T(8,128)S(1)} %fusion.29, f32[8,8]{0,1:T(8,128)S(1)} %fusion.30, f32[8,8]{0,1:T(8,128)S(1)} %fusion.31), channel_id=1, replica_groups=mesh['gx'=4,'gy'=8,'gz'=8] {'gx','gy','gz'}, use_global_device_ids=true, to_apply=%region_1.0 | all-reduce | flops 256 | bytes 2048 | tf_op jit(solution)/shard_map/psum | solution.py:81
  368.8 74.7 %all-reduce.1 = (f32[128,8]{0,1:T(8,128)S(1)}, f32[128,8]{0,1:T(8,128)S(1)}, f32[128,8]{0,1:T(8,128)S(1)}, f32[128,8]{0,1:T(8,128)S(1)}) all-reduce(f32[128,8]{0,1:T(8,128)S(1)} %fusion.23, f32[128,8]{0,1:T(8,128)S(1)} %fusion.11, f32[128,8]{0,1:T(8,128)S(1)} %fusion.15, ...), channel_id=1, replica_groups=mesh['gx'=4,'gy'=8,'gz'=8] {'gx','gy','gz'}, use_global_device_ids=true, to_apply=%region_4.0 | all-reduce | flops 4096 | bytes 32768 | tf_op jit(solution)/shard_map/psum | solution.py:84
  447.7 73.6 %all-reduce = (f32[8,8]{0,1:T(8,128)S(1)}, f32[8,8]{0,1:T(8,128)S(1)}, f32[8,8]{0,1:T(8,128)S(1)}, f32[8,8]{0,1:T(8,128)S(1)}) all-reduce(f32[8,8]{0,1:T(8,128)S(1)} %fusion.32, f32[8,8]{0,1:T(8,128)S(1)} %fusion.26, f32[8,8]{0,1:T(8,128)S(1)} %fusion.27, f32[8,8]{0,1:T(8,128)S(1)} %fusion.28), channel_id=1, replica_groups=mesh['gx'=4,'gy'=8,'gz'=8] {'gx','gy','gz'}, use_global_device_ids=true, to_apply=%region_5.0 | all-reduce | flops 256 | bytes 2048 | tf_op jit(solution)/shard_map/psum | solution.py:88
  (208 shorter events, 106.6 us)
Async XLA Ops:
  0.6 7.2 %copy-start = (bf16[2,3,8,128,128]{4,3,2,1,0:T(8,128)(2,1)S(1)}, bf16[2,3,8,128,128]{4,3,2,1,0:T(8,128)(2,1)}, u32[]{:S(2)}) copy-start(bf16[2,3,8,128,128]{4,3,2,1,0:T(8,128)(2,1)} %param.10) | copy-start | bytes 4718596
  2.5 23.6 %collective-permute-start = (f32[11,2,8,128]{3,2,1,0:T(8,128)S(1)}, f32[11,2,8,128]{3,2,1,0:T(8,128)S(1)}, u32[]{:S(2)}, u32[]{:S(2)}) collective-permute-start(f32[11,2,8,128]{3,2,1,0:T(8,128)S(1)} %pad_maximum_fusion.10), channel_id=1, source_target_pairs={{0,64},{64,128},{128,192},{1,65},{65,129},{129,193},{2,66},{66,130... | collective-permute-start | bytes 270344 | tf_op jit(solution)/shard_map/ppermute | solution.py:16
  6.5 19.6 %collective-permute-start.1 = (f32[11,2,8,128]{3,2,1,0:T(8,128)S(1)}, f32[11,2,8,128]{3,2,1,0:T(8,128)S(1)}, u32[]{:S(2)}, u32[]{:S(2)}) collective-permute-start(f32[11,2,8,128]{3,2,1,0:T(8,128)S(1)} %pad_maximum_fusion.10), channel_id=1, source_target_pairs={{64,0},{128,64},{192,128},{65,1},{129,65},{193,129},{66,2},{130,66... | collective-permute-start | bytes 270344 | tf_op jit(solution)/shard_map/ppermute | solution.py:19
  9.1 5.6 %collective-permute-start.6 = (f32[3,8,1,8,128]{4,1,3,2,0:T(8,128)S(1)}, f32[3,8,1,8,128]{4,1,3,2,0:T(8,128)S(1)}, u32[]{:S(2)}, u32[]{:S(2)}) collective-permute-start(f32[3,8,1,8,128]{4,1,3,2,0:T(8,128)S(1)} %copy.383), channel_id=1, source_target_pairs={{0,64},{64,128},{128,192},{1,65},{65,129},{129,193},{2,66},{66,130... | collective-permute-start | bytes 294920 | tf_op jit(solution)/shard_map/ppermute | solution.py:16
  13.1 5.4 collective-permute-start.7
  18.5 7.7 %collective-permute-start.8 = (f32[3,8,4,1,128]{4,1,3,2,0:T(8,128)S(1)}, f32[3,8,4,1,128]{4,1,3,2,0:T(8,128)S(1)}, u32[]{:S(2)}, u32[]{:S(2)}) collective-permute-start(f32[3,8,4,1,128]{4,1,3,2,0:T(8,128)S(1)} %get-tuple-element.78), channel_id=1, source_target_pairs={{0,8},{8,16},{16,24},{24,32},{32,40},{40,48},{48,56},{1,9},{9,17},... | collective-permute-start | bytes 147464 | tf_op jit(solution)/shard_map/ppermute | solution.py:16
  24.2 5.4 %collective-permute-start.9 = (f32[3,8,4,1,128]{4,1,3,2,0:T(8,128)S(1)}, f32[3,8,4,1,128]{4,1,3,2,0:T(8,128)S(1)}, u32[]{:S(2)}, u32[]{:S(2)}) collective-permute-start(f32[3,8,4,1,128]{4,1,3,2,0:T(8,128)S(1)} %get-tuple-element.79), channel_id=1, source_target_pairs={{8,0},{16,8},{24,16},{32,24},{40,32},{48,40},{56,48},{9,1},{17,9},... | collective-permute-start | bytes 147464 | tf_op jit(solution)/shard_map/ppermute | solution.py:19
  30.7 14.4 %collective-permute-start.10 = (f32[3,8,4,10,1]{4,1,3,2,0:T(8,128)}, f32[3,8,4,10,1]{4,1,3,2,0:T(8,128)S(1)}, u32[]{:S(2)}, u32[]{:S(2)}) collective-permute-start(f32[3,8,4,10,1]{4,1,3,2,0:T(8,128)} %get-tuple-element.70), channel_id=1, source_target_pairs={{0,1},{1,2},{2,3},{3,4},{4,5},{5,6},{6,7},{8,9},{9,10},{10,11},{11... | collective-permute-start | bytes 11528 | tf_op jit(solution)/shard_map/ppermute | solution.py:16
  34.3 13.6 %collective-permute-start.11 = (f32[3,8,4,10,1]{4,1,3,2,0:T(8,128)}, f32[3,8,4,10,1]{4,1,3,2,0:T(8,128)}, u32[]{:S(2)}, u32[]{:S(2)}) collective-permute-start(f32[3,8,4,10,1]{4,1,3,2,0:T(8,128)} %get-tuple-element.71), channel_id=1, source_target_pairs={{1,0},{2,1},{3,2},{4,3},{5,4},{6,5},{7,6},{9,8},{10,9},{11,10},{12... | collective-permute-start | bytes 11528 | tf_op jit(solution)/shard_map/ppermute | solution.py:19
  39.5 10.1 %collective-permute-start.2 = (f32[11,6,2,128]{3,1,2,0:T(8,128)S(1)}, f32[11,6,2,128]{3,1,2,0:T(8,128)}, u32[]{:S(2)}, u32[]{:S(2)}) collective-permute-start(f32[11,6,2,128]{3,1,2,0:T(8,128)S(1)} %copy.326), channel_id=1, source_target_pairs={{0,8},{8,16},{16,24},{24,32},{32,40},{40,48},{48,56},{1,9},{9,17},... | collective-permute-start | bytes 202760 | tf_op jit(solution)/shard_map/ppermute | solution.py:16
  42.3 11.8 %collective-permute-start.3 = (f32[11,6,2,128]{3,1,2,0:T(8,128)}, f32[11,6,2,128]{3,1,2,0:T(8,128)S(1)}, u32[]{:S(2)}, u32[]{:S(2)}) collective-permute-start(f32[11,6,2,128]{3,1,2,0:T(8,128)} %copy.327), channel_id=1, source_target_pairs={{8,0},{16,8},{24,16},{32,24},{40,32},{48,40},{56,48},{9,1},{17,9},... | collective-permute-start | bytes 202760 | tf_op jit(solution)/shard_map/ppermute | solution.py:19
  69.5 10.0 %collective-permute-start.4 = (f32[11,6,12,2]{2,1,3,0:T(8,128)S(1)}, f32[11,6,12,2]{2,1,3,0:T(8,128)S(1)}, u32[]{:S(2)}, u32[]{:S(2)}) collective-permute-start(f32[11,6,12,2]{2,1,3,0:T(8,128)S(1)} %get-tuple-element.44), channel_id=1, source_target_pairs={{0,1},{1,2},{2,3},{3,4},{4,5},{5,6},{6,7},{8,9},{9,10},{10,11},{11... | collective-permute-start | bytes 19016 | tf_op jit(solution)/shard_map/ppermute | solution.py:16
  73.1 7.0 %collective-permute-start.5 = (f32[11,6,12,2]{2,1,3,0:T(8,128)S(1)}, f32[11,6,12,2]{2,1,3,0:T(8,128)S(1)}, u32[]{:S(2)}, u32[]{:S(2)}) collective-permute-start(f32[11,6,12,2]{2,1,3,0:T(8,128)S(1)} %get-tuple-element.45), channel_id=1, source_target_pairs={{1,0},{2,1},{3,2},{4,3},{5,4},{6,5},{7,6},{9,8},{10,9},{11,10},{12... | collective-permute-start | bytes 19016 | tf_op jit(solution)/shard_map/ppermute | solution.py:19
  81.4 4.3 copy-start.4
  86.2 5.6 %collective-permute-start.12 = (f32[3,8,1,8,128]{4,1,3,2,0:T(8,128)S(1)}, f32[3,8,1,8,128]{4,1,3,2,0:T(8,128)S(1)}, u32[]{:S(2)}, u32[]{:S(2)}) collective-permute-start(f32[3,8,1,8,128]{4,1,3,2,0:T(8,128)S(1)} %get-tuple-element.86), channel_id=1, source_target_pairs={{0,64},{64,128},{128,192},{1,65},{65,129},{129,193},{2,66},{66,130... | collective-permute-start | bytes 294920 | tf_op jit(solution)/shard_map/ppermute | solution.py:16
  89.4 6.2 %collective-permute-start.13 = (f32[3,8,1,8,128]{4,1,3,2,0:T(8,128)S(1)}, f32[3,8,1,8,128]{4,1,3,2,0:T(8,128)S(1)}, u32[]{:S(2)}, u32[]{:S(2)}) collective-permute-start(f32[3,8,1,8,128]{4,1,3,2,0:T(8,128)S(1)} %get-tuple-element.87), channel_id=1, source_target_pairs={{64,0},{128,64},{192,128},{65,1},{129,65},{193,129},{66,2},{130,66... | collective-permute-start | bytes 294920 | tf_op jit(solution)/shard_map/ppermute | solution.py:19
  95.6 7.9 %collective-permute-start.14 = (f32[3,8,4,1,128]{4,1,3,2,0:T(8,128)S(1)}, f32[3,8,4,1,128]{4,1,3,2,0:T(8,128)S(1)}, u32[]{:S(2)}, u32[]{:S(2)}) collective-permute-start(f32[3,8,4,1,128]{4,1,3,2,0:T(8,128)S(1)} %get-tuple-element.76), channel_id=1, source_target_pairs={{0,8},{8,16},{16,24},{24,32},{32,40},{40,48},{48,56},{1,9},{9,17},... | collective-permute-start | bytes 147464 | tf_op jit(solution)/shard_map/ppermute | solution.py:16
  101.6 5.4 %collective-permute-start.15 = (f32[3,8,4,1,128]{4,1,3,2,0:T(8,128)S(1)}, f32[3,8,4,1,128]{4,1,3,2,0:T(8,128)S(1)}, u32[]{:S(2)}, u32[]{:S(2)}) collective-permute-start(f32[3,8,4,1,128]{4,1,3,2,0:T(8,128)S(1)} %get-tuple-element.77), channel_id=1, source_target_pairs={{8,0},{16,8},{24,16},{32,24},{40,32},{48,40},{56,48},{9,1},{17,9},... | collective-permute-start | bytes 147464 | tf_op jit(solution)/shard_map/ppermute | solution.py:19
  107.2 14.1 %collective-permute-start.16 = (f32[3,8,4,10,1]{4,1,3,2,0:T(8,128)S(1)}, f32[3,8,4,10,1]{4,1,3,2,0:T(8,128)S(1)}, u32[]{:S(2)}, u32[]{:S(2)}) collective-permute-start(f32[3,8,4,10,1]{4,1,3,2,0:T(8,128)S(1)} %get-tuple-element.68), channel_id=1, source_target_pairs={{0,1},{1,2},{2,3},{3,4},{4,5},{5,6},{6,7},{8,9},{9,10},{10,11},{11... | collective-permute-start | bytes 11528 | tf_op jit(solution)/shard_map/ppermute | solution.py:16
  112.1 14.4 %collective-permute-start.17 = (f32[3,8,4,10,1]{4,1,3,2,0:T(8,128)S(1)}, f32[3,8,4,10,1]{4,1,3,2,0:T(8,128)S(1)}, u32[]{:S(2)}, u32[]{:S(2)}) collective-permute-start(f32[3,8,4,10,1]{4,1,3,2,0:T(8,128)S(1)} %get-tuple-element.69), channel_id=1, source_target_pairs={{1,0},{2,1},{3,2},{4,3},{5,4},{6,5},{7,6},{9,8},{10,9},{11,10},{12... | collective-permute-start | bytes 11528 | tf_op jit(solution)/shard_map/ppermute | solution.py:19
  127.7 4.8 collective-permute-start.18
  130.7 6.0 %collective-permute-start.19 = (f32[3,8,1,8,128]{4,1,3,2,0:T(8,128)S(1)}, f32[3,8,1,8,128]{4,1,3,2,0:T(8,128)S(1)}, u32[]{:S(2)}, u32[]{:S(2)}) collective-permute-start(f32[3,8,1,8,128]{4,1,3,2,0:T(8,128)S(1)} %copy.386), channel_id=1, source_target_pairs={{64,0},{128,64},{192,128},{65,1},{129,65},{193,129},{66,2},{130,66... | collective-permute-start | bytes 294920 | tf_op jit(solution)/shard_map/ppermute | solution.py:19
  136.7 7.2 %collective-permute-start.20 = (f32[3,8,4,1,128]{4,1,3,2,0:T(8,128)S(1)}, f32[3,8,4,1,128]{4,1,3,2,0:T(8,128)S(1)}, u32[]{:S(2)}, u32[]{:S(2)}) collective-permute-start(f32[3,8,4,1,128]{4,1,3,2,0:T(8,128)S(1)} %get-tuple-element.74), channel_id=1, source_target_pairs={{0,8},{8,16},{16,24},{24,32},{32,40},{40,48},{48,56},{1,9},{9,17},... | collective-permute-start | bytes 147464 | tf_op jit(solution)/shard_map/ppermute | solution.py:16
  142.0 5.4 %collective-permute-start.21 = (f32[3,8,4,1,128]{4,1,3,2,0:T(8,128)S(1)}, f32[3,8,4,1,128]{4,1,3,2,0:T(8,128)S(1)}, u32[]{:S(2)}, u32[]{:S(2)}) collective-permute-start(f32[3,8,4,1,128]{4,1,3,2,0:T(8,128)S(1)} %get-tuple-element.75), channel_id=1, source_target_pairs={{8,0},{16,8},{24,16},{32,24},{40,32},{48,40},{56,48},{9,1},{17,9},... | collective-permute-start | bytes 147464 | tf_op jit(solution)/shard_map/ppermute | solution.py:19
  147.6 12.9 %collective-permute-start.22 = (f32[3,8,4,10,1]{4,1,3,2,0:T(8,128)S(1)}, f32[3,8,4,10,1]{4,1,3,2,0:T(8,128)S(1)}, u32[]{:S(2)}, u32[]{:S(2)}) collective-permute-start(f32[3,8,4,10,1]{4,1,3,2,0:T(8,128)S(1)} %get-tuple-element.66), channel_id=1, source_target_pairs={{0,1},{1,2},{2,3},{3,4},{4,5},{5,6},{6,7},{8,9},{9,10},{10,11},{11... | collective-permute-start | bytes 11528 | tf_op jit(solution)/shard_map/ppermute | solution.py:16
  151.3 13.3 %collective-permute-start.23 = (f32[3,8,4,10,1]{4,1,3,2,0:T(8,128)S(1)}, f32[3,8,4,10,1]{4,1,3,2,0:T(8,128)S(1)}, u32[]{:S(2)}, u32[]{:S(2)}) collective-permute-start(f32[3,8,4,10,1]{4,1,3,2,0:T(8,128)S(1)} %get-tuple-element.67), channel_id=1, source_target_pairs={{1,0},{2,1},{3,2},{4,3},{5,4},{6,5},{7,6},{9,8},{10,9},{11,10},{12... | collective-permute-start | bytes 11528 | tf_op jit(solution)/shard_map/ppermute | solution.py:19
  165.8 3.8 collective-permute-start.24
  167.7 6.0 %collective-permute-start.25 = (f32[3,8,1,8,128]{4,1,3,2,0:T(8,128)S(1)}, f32[3,8,1,8,128]{4,1,3,2,0:T(8,128)S(1)}, u32[]{:S(2)}, u32[]{:S(2)}) collective-permute-start(f32[3,8,1,8,128]{4,1,3,2,0:T(8,128)S(1)} %get-tuple-element.83), channel_id=1, source_target_pairs={{64,0},{128,64},{192,128},{65,1},{129,65},{193,129},{66,2},{130,66... | collective-permute-start | bytes 294920 | tf_op jit(solution)/shard_map/ppermute | solution.py:19
  173.7 7.0 %collective-permute-start.26 = (f32[3,8,4,1,128]{4,1,3,2,0:T(8,128)S(1)}, f32[3,8,4,1,128]{4,1,3,2,0:T(8,128)S(1)}, u32[]{:S(2)}, u32[]{:S(2)}) collective-permute-start(f32[3,8,4,1,128]{4,1,3,2,0:T(8,128)S(1)} %get-tuple-element.72), channel_id=1, source_target_pairs={{0,8},{8,16},{16,24},{24,32},{32,40},{40,48},{48,56},{1,9},{9,17},... | collective-permute-start | bytes 147464 | tf_op jit(solution)/shard_map/ppermute | solution.py:16
  178.5 5.4 %collective-permute-start.27 = (f32[3,8,4,1,128]{4,1,3,2,0:T(8,128)S(1)}, f32[3,8,4,1,128]{4,1,3,2,0:T(8,128)S(1)}, u32[]{:S(2)}, u32[]{:S(2)}) collective-permute-start(f32[3,8,4,1,128]{4,1,3,2,0:T(8,128)S(1)} %get-tuple-element.73), channel_id=1, source_target_pairs={{8,0},{16,8},{24,16},{32,24},{40,32},{48,40},{56,48},{9,1},{17,9},... | collective-permute-start | bytes 147464 | tf_op jit(solution)/shard_map/ppermute | solution.py:19
  184.2 13.8 %collective-permute-start.28 = (f32[3,8,4,10,1]{4,1,3,2,0:T(8,128)S(1)}, f32[3,8,4,10,1]{4,1,3,2,0:T(8,128)S(1)}, u32[]{:S(2)}, u32[]{:S(2)}) collective-permute-start(f32[3,8,4,10,1]{4,1,3,2,0:T(8,128)S(1)} %get-tuple-element.64), channel_id=1, source_target_pairs={{0,1},{1,2},{2,3},{3,4},{4,5},{5,6},{6,7},{8,9},{9,10},{10,11},{11... | collective-permute-start | bytes 11528 | tf_op jit(solution)/shard_map/ppermute | solution.py:16
  188.8 13.3 %collective-permute-start.29 = (f32[3,8,4,10,1]{4,1,3,2,0:T(8,128)S(1)}, f32[3,8,4,10,1]{4,1,3,2,0:T(8,128)S(1)}, u32[]{:S(2)}, u32[]{:S(2)}) collective-permute-start(f32[3,8,4,10,1]{4,1,3,2,0:T(8,128)S(1)} %get-tuple-element.65), channel_id=1, source_target_pairs={{1,0},{2,1},{3,2},{4,3},{5,4},{6,5},{7,6},{9,8},{10,9},{11,10},{12... | collective-permute-start | bytes 11528 | tf_op jit(solution)/shard_map/ppermute | solution.py:19
  (3 other events, 7.5 us)
where the time goes:
time: 540 us; the launch traced here: 538 us
  blocking collectives  295 us (55%)
  starting transfers between devices  83.7 us (16%)
  waiting for transfers between devices  70.1 us (13%)
  other arithmetic  38.1 us (7%)
  local copies, waits for them, and re-layouts  27.4 us (5%)
  matrix products  22 us (4%)
    psum x1, blocking collectives, orthonormalize(): lax.psum(project(basis, first_q.astype(jnp.bfloat16)) * dof_weight, ('gx'...  74.7 us
    psum x1, blocking collectives, orthonormalize(): first_coef = lax.psum(partial_coef, ('gx', 'gy', 'gz'))  73.7 us
    psum x1, blocking collectives, orthonormalize(): lax.psum(local_gram(second_resid) * dof_weight, ('gx', 'gy', 'gz'))  73.6 us
    psum x1, blocking collectives, orthonormalize(): lax.psum(local_gram(first_resid) * dof_weight, ('gx', 'gy', 'gz'))  73 us
    ppermute x15, starting transfers between devices, padded_2(): lax.ppermute(lax.slice_in_dim(block, block.shape[dim] - width, None, axis...  60.2 us
    ppermute x15, waiting for transfers between devices, padded_2(): lax.ppermute(lax.slice_in_dim(block, 0, width, axis=dim), axis, backward)  44.8 us
    ppermute x15, waiting for transfers between devices, padded_2(): lax.ppermute(lax.slice_in_dim(block, block.shape[dim] - width, None, axis...  25.3 us
    ppermute x15, starting transfers between devices, padded_2(): lax.ppermute(lax.slice_in_dim(block, 0, width, axis=dim), axis, backward)  23.6 us
  transfers between devices with their start and end apart: 30, of which 19 were waited for; matrix products, arithmetic and copies ran while one was open for 3% of the time, Pallas kernels for 0%

commit v1 on v0

--- a/solution.py
+++ b/solution.py
@@ -76,7 +76,7 @@
     highest = lax.Precision.HIGHEST
     snapshot = following.astype(jnp.bfloat16)
     partial_coef = project(basis, snapshot) * dof_weight
-    first_coef = lax.psum(partial_coef, ("gx", "gy", "gz"))
+    first_coef = lax.psum(lax.psum(partial_coef, ("gy", "gz")), "gx")
     first_resid = snapshot.astype(jnp.float32) - expand(basis, first_coef.astype(jnp.bfloat16))
     first_gram = lax.psum(local_gram(first_resid) * dof_weight, ("gx", "gy", "gz"))
     first_lower = jnp.linalg.cholesky(first_gram)

time: 540 us -> 725 us (1.34)
  blocking collectives: 295 us -> 481 us
    psum x1 -> x2, blocking collectives: 73.7 us -> 249 us  [orthonormalize(): first_coef = lax.psum(lax.psum(partial_coef, ('gy', 'gz')), 'gx')]
    psum x1, blocking collectives: 73 us -> 83.9 us  [orthonormalize(): lax.psum(local_gram(first_resid) * dof_weight, ('gx', 'gy', 'gz'))]
where the time goes in v1:
time: 725 us; the launch traced here: 724 us
  blocking collectives  481 us (66%)
  starting transfers between devices  83.7 us (12%)
  waiting for transfers between devices  70.1 us (10%)
  other arithmetic  38.2 us (5%)
  local copies, waits for them, and re-layouts  27.3 us (4%)
  matrix products  21.9 us (3%)
    psum x2, blocking collectives, orthonormalize(): first_coef = lax.psum(lax.psum(partial_coef, ('gy', 'gz')), 'gx')  249 us
    psum x1, blocking collectives, orthonormalize(): lax.psum(local_gram(first_resid) * dof_weight, ('gx', 'gy', 'gz'))  83.9 us
    psum x1, blocking collectives, orthonormalize(): lax.psum(project(basis, first_q.astype(jnp.bfloat16)) * dof_weight, ('gx'...  74.6 us
    psum x1, blocking collectives, orthonormalize(): lax.psum(local_gram(second_resid) * dof_weight, ('gx', 'gy', 'gz'))  73.6 us
    ppermute x15, starting transfers between devices, padded_2(): lax.ppermute(lax.slice_in_dim(block, block.shape[dim] - width, None, axis...  60.1 us
    ppermute x15, waiting for transfers between devices, padded_2(): lax.ppermute(lax.slice_in_dim(block, 0, width, axis=dim), axis, backward)  44.9 us
    ppermute x15, waiting for transfers between devices, padded_2(): lax.ppermute(lax.slice_in_dim(block, block.shape[dim] - width, None, axis...  25.3 us
    ppermute x15, starting transfers between devices, padded_2(): lax.ppermute(lax.slice_in_dim(block, 0, width, axis=dim), axis, backward)  23.6 us
  transfers between devices with their start and end apart: 30, of which 19 were waited for; matrix products, arithmetic and copies ran while one was open for 3% of the time, Pallas kernels for 0%

profile of v1, /device:TPU:1, one launch (start us, length us, event | category | flops | bytes accessed | tf_op | source)
XLA Modules:
  0.0 723.6 jit_solution(14797789047870490768)
XLA Ops:
  2.5 4.0 collective-permute-start
  9.1 4.0 collective-permute-start.6
  14.7 3.7 collective-permute-done.7
  18.5 5.7 collective-permute-start.8
  30.7 3.6 collective-permute-start.10
  35.7 3.8 copy.222
  49.6 4.5 copy.221
  54.1 3.9 copy.223
  58.0 9.0 %pad_maximum_fusion = f32[11,6,12,128]{2,1,3,0:T(8,128)S(1)} fusion(f32[11,6,2,128]{2,1,3,0:T(8,128)} %copy.223, f32[11,6,8,128]{2,1,3,0:T(8,128)} %copy.222, f32[11,6,2,128]{2,1,3,0:T(8,128)} %copy.221), kind=kLoop, calls=%fused_computation | loop fusion | flops 202752 | bytes 811008 | tf_op jit(solution)/shard_map/concatenate | solution.py:20
  69.5 3.5 collective-permute-start.4
  75.3 4.2 copy.225
  91.9 3.9 collective-permute-done.13
  95.9 5.9 collective-permute-start.14
  103.7 3.5 collective-permute-done.15
  107.4 4.9 collective-permute-start.16
  113.6 7.9 %collective-permute-done.16 = f32[3,8,4,10,1]{4,1,3,2,0:T(8,128)S(1)} collective-permute-done((f32[3,8,4,10,1]{4,1,3,2,0:T(8,128)S(1)}, f32[3,8,4,10,1]{4,1,3,2,0:T(8,128)S(1)}, u32[]{:S(2)}, u32[]{:S(2)}) %collective-permute-start.16) | collective-permute-done | bytes 3872 | tf_op jit(solution)/shard_map/ppermute | solution.py:16
  121.5 5.2 collective-permute-done.17
  132.7 4.1 collective-permute-done.19
  136.8 5.3 collective-permute-start.20
  147.8 3.7 collective-permute-start.22
  153.0 7.7 %collective-permute-done.22 = f32[3,8,4,10,1]{4,1,3,2,0:T(8,128)S(1)} collective-permute-done((f32[3,8,4,10,1]{4,1,3,2,0:T(8,128)S(1)}, f32[3,8,4,10,1]{4,1,3,2,0:T(8,128)S(1)}, u32[]{:S(2)}, u32[]{:S(2)}) %collective-permute-start.22) | collective-permute-done | bytes 3872 | tf_op jit(solution)/shard_map/ppermute | solution.py:16
  160.7 4.1 collective-permute-done.23
  169.8 4.1 collective-permute-done.25
  173.9 4.8 collective-permute-start.26
  184.3 4.6 collective-permute-start.28
  190.6 7.6 %collective-permute-done.28 = f32[3,8,4,10,1]{4,1,3,2,0:T(8,128)S(1)} collective-permute-done((f32[3,8,4,10,1]{4,1,3,2,0:T(8,128)S(1)}, f32[3,8,4,10,1]{4,1,3,2,0:T(8,128)S(1)}, u32[]{:S(2)}, u32[]{:S(2)}) %collective-permute-start.28) | collective-permute-done | bytes 3872 | tf_op jit(solution)/shard_map/ppermute | solution.py:16
  198.1 4.1 collective-permute-done.29
  203.7 238.0 %all-reduce.3 = (f32[128,8]{0,1:T(8,128)S(1)}, f32[128,8]{0,1:T(8,128)S(1)}, f32[128,8]{0,1:T(8,128)S(1)}, f32[128,8]{0,1:T(8,128)S(1)}) all-reduce(f32[128,8]{0,1:T(8,128)S(1)} %fusion.25, f32[128,8]{0,1:T(8,128)S(1)} %fusion.13, f32[128,8]{0,1:T(8,128)S(1)} %fusion.17, ...), channel_id=1, replica_groups=mesh['gx'=4,'gy'=8,'gz'=8] {'gy','gz'}, use_global_device_ids=true, to_apply=%region_0.0 | all-reduce | flops 4096 | bytes 32768 | tf_op jit(solution)/shard_map/psum | solution.py:79
  441.7 10.8 %all-reduce.4 = (f32[128,8]{0,1:T(8,128)S(1)}, f32[128,8]{0,1:T(8,128)S(1)}, f32[128,8]{0,1:T(8,128)S(1)}, f32[128,8]{0,1:T(8,128)S(1)}) all-reduce(f32[128,8]{0,1:T(8,128)S(1)} %get-tuple-element.34, f32[128,8]{0,1:T(8,128)S(1)} %get-tuple-element.35, ...), channel_id=1, replica_groups=mesh['gx'=4,'gy'=8,'gz'=8] {'gx'}, use_global_device_ids=true, to_apply=%region_1.0 | all-reduce | flops 4096 | bytes 32768 | tf_op jit(solution)/shard_map/psum | solution.py:79
  456.7 83.9 %all-reduce.2 = (f32[8,8]{0,1:T(8,128)S(1)}, f32[8,8]{0,1:T(8,128)S(1)}, f32[8,8]{0,1:T(8,128)S(1)}, f32[8,8]{0,1:T(8,128)S(1)}) all-reduce(f32[8,8]{0,1:T(8,128)S(1)} %fusion.33, f32[8,8]{0,1:T(8,128)S(1)} %fusion.29, f32[8,8]{0,1:T(8,128)S(1)} %fusion.30, f32[8,8]{0,1:T(8,128)S(1)} %fusion.31), channel_id=1, replica_groups=mesh['gx'=4,'gy'=8,'gz'=8] {'gx','gy','gz'}, use_global_device_ids=true, to_apply=%region_2.0 | all-reduce | flops 256 | bytes 2048 | tf_op jit(solution)/shard_map/psum | solution.py:81
  554.9 74.6 %all-reduce.1 = (f32[128,8]{0,1:T(8,128)S(1)}, f32[128,8]{0,1:T(8,128)S(1)}, f32[128,8]{0,1:T(8,128)S(1)}, f32[128,8]{0,1:T(8,128)S(1)}) all-reduce(f32[128,8]{0,1:T(8,128)S(1)} %fusion.23, f32[128,8]{0,1:T(8,128)S(1)} %fusion.11, f32[128,8]{0,1:T(8,128)S(1)} %fusion.15, ...), channel_id=1, replica_groups=mesh['gx'=4,'gy'=8,'gz'=8] {'gx','gy','gz'}, use_global_device_ids=true, to_apply=%region_5.0 | all-reduce | flops 4096 | bytes 32768 | tf_op jit(solution)/shard_map/psum | solution.py:84
  633.7 73.6 %all-reduce = (f32[8,8]{0,1:T(8,128)S(1)}, f32[8,8]{0,1:T(8,128)S(1)}, f32[8,8]{0,1:T(8,128)S(1)}, f32[8,8]{0,1:T(8,128)S(1)}) all-reduce(f32[8,8]{0,1:T(8,128)S(1)} %fusion.32, f32[8,8]{0,1:T(8,128)S(1)} %fusion.26, f32[8,8]{0,1:T(8,128)S(1)} %fusion.27, f32[8,8]{0,1:T(8,128)S(1)} %fusion.28), channel_id=1, replica_groups=mesh['gx'=4,'gy'=8,'gz'=8] {'gx','gy','gz'}, use_global_device_ids=true, to_apply=%region_6.0 | all-reduce | flops 256 | bytes 2048 | tf_op jit(solution)/shard_map/psum | solution.py:88
  (209 shorter events, 110.0 us)
Async XLA Ops:
  0.6 7.2 copy-start
  2.5 23.6 %collective-permute-start = (f32[11,2,8,128]{3,2,1,0:T(8,128)S(1)}, f32[11,2,8,128]{3,2,1,0:T(8,128)S(1)}, u32[]{:S(2)}, u32[]{:S(2)}) collective-permute-start(f32[11,2,8,128]{3,2,1,0:T(8,128)S(1)} %pad_maximum_fusion.10), channel_id=1, source_target_pairs={{0,64},{64,128},{128,192},{1,65},{65,129},{129,193},{2,66},{66,130... | collective-permute-start | bytes 270344 | tf_op jit(solution)/shard_map/ppermute | solution.py:16
  6.5 19.6 %collective-permute-start.1 = (f32[11,2,8,128]{3,2,1,0:T(8,128)S(1)}, f32[11,2,8,128]{3,2,1,0:T(8,128)S(1)}, u32[]{:S(2)}, u32[]{:S(2)}) collective-permute-start(f32[11,2,8,128]{3,2,1,0:T(8,128)S(1)} %pad_maximum_fusion.10), channel_id=1, source_target_pairs={{64,0},{128,64},{192,128},{65,1},{129,65},{193,129},{66,2},{130,66... | collective-permute-start | bytes 270344 | tf_op jit(solution)/shard_map/ppermute | solution.py:19
  9.1 5.6 collective-permute-start.6
  13.1 5.4 collective-permute-start.7
  18.5 7.7 %collective-permute-start.8 = (f32[3,8,4,1,128]{4,1,3,2,0:T(8,128)S(1)}, f32[3,8,4,1,128]{4,1,3,2,0:T(8,128)S(1)}, u32[]{:S(2)}, u32[]{:S(2)}) collective-permute-start(f32[3,8,4,1,128]{4,1,3,2,0:T(8,128)S(1)} %get-tuple-element.82), channel_id=1, source_target_pairs={{0,8},{8,16},{16,24},{24,32},{32,40},{40,48},{48,56},{1,9},{9,17},... | collective-permute-start | bytes 147464 | tf_op jit(solution)/shard_map/ppermute | solution.py:16
  24.2 5.4 collective-permute-start.9
  30.7 14.4 %collective-permute-start.10 = (f32[3,8,4,10,1]{4,1,3,2,0:T(8,128)}, f32[3,8,4,10,1]{4,1,3,2,0:T(8,128)S(1)}, u32[]{:S(2)}, u32[]{:S(2)}) collective-permute-start(f32[3,8,4,10,1]{4,1,3,2,0:T(8,128)} %get-tuple-element.74), channel_id=1, source_target_pairs={{0,1},{1,2},{2,3},{3,4},{4,5},{5,6},{6,7},{8,9},{9,10},{10,11},{11... | collective-permute-start | bytes 11528 | tf_op jit(solution)/shard_map/ppermute | solution.py:16
  34.3 13.6 %collective-permute-start.11 = (f32[3,8,4,10,1]{4,1,3,2,0:T(8,128)}, f32[3,8,4,10,1]{4,1,3,2,0:T(8,128)}, u32[]{:S(2)}, u32[]{:S(2)}) collective-permute-start(f32[3,8,4,10,1]{4,1,3,2,0:T(8,128)} %get-tuple-element.75), channel_id=1, source_target_pairs={{1,0},{2,1},{3,2},{4,3},{5,4},{6,5},{7,6},{9,8},{10,9},{11,10},{12... | collective-permute-start | bytes 11528 | tf_op jit(solution)/shard_map/ppermute | solution.py:19
  39.5 10.1 %collective-permute-start.2 = (f32[11,6,2,128]{3,1,2,0:T(8,128)S(1)}, f32[11,6,2,128]{3,1,2,0:T(8,128)}, u32[]{:S(2)}, u32[]{:S(2)}) collective-permute-start(f32[11,6,2,128]{3,1,2,0:T(8,128)S(1)} %copy.326), channel_id=1, source_target_pairs={{0,8},{8,16},{16,24},{24,32},{32,40},{40,48},{48,56},{1,9},{9,17},... | collective-permute-start | bytes 202760 | tf_op jit(solution)/shard_map/ppermute | solution.py:16
  42.3 11.8 %collective-permute-start.3 = (f32[11,6,2,128]{3,1,2,0:T(8,128)}, f32[11,6,2,128]{3,1,2,0:T(8,128)S(1)}, u32[]{:S(2)}, u32[]{:S(2)}) collective-permute-start(f32[11,6,2,128]{3,1,2,0:T(8,128)} %copy.327), channel_id=1, source_target_pairs={{8,0},{16,8},{24,16},{32,24},{40,32},{48,40},{56,48},{9,1},{17,9},... | collective-permute-start | bytes 202760 | tf_op jit(solution)/shard_map/ppermute | solution.py:19
  69.5 10.0 %collective-permute-start.4 = (f32[11,6,12,2]{2,1,3,0:T(8,128)S(1)}, f32[11,6,12,2]{2,1,3,0:T(8,128)S(1)}, u32[]{:S(2)}, u32[]{:S(2)}) collective-permute-start(f32[11,6,12,2]{2,1,3,0:T(8,128)S(1)} %get-tuple-element.48), channel_id=1, source_target_pairs={{0,1},{1,2},{2,3},{3,4},{4,5},{5,6},{6,7},{8,9},{9,10},{10,11},{11... | collective-permute-start | bytes 19016 | tf_op jit(solution)/shard_map/ppermute | solution.py:16
  73.0 7.0 collective-permute-start.5
  81.3 4.5 copy-start.4
  86.4 5.5 collective-permute-start.12
  89.6 6.3 collective-permute-start.13
  95.9 7.9 %collective-permute-start.14 = (f32[3,8,4,1,128]{4,1,3,2,0:T(8,128)S(1)}, f32[3,8,4,1,128]{4,1,3,2,0:T(8,128)S(1)}, u32[]{:S(2)}, u32[]{:S(2)}) collective-permute-start(f32[3,8,4,1,128]{4,1,3,2,0:T(8,128)S(1)} %get-tuple-element.80), channel_id=1, source_target_pairs={{0,8},{8,16},{16,24},{24,32},{32,40},{40,48},{48,56},{1,9},{9,17},... | collective-permute-start | bytes 147464 | tf_op jit(solution)/shard_map/ppermute | solution.py:16
  101.8 5.4 collective-permute-start.15
  107.4 14.1 %collective-permute-start.16 = (f32[3,8,4,10,1]{4,1,3,2,0:T(8,128)S(1)}, f32[3,8,4,10,1]{4,1,3,2,0:T(8,128)S(1)}, u32[]{:S(2)}, u32[]{:S(2)}) collective-permute-start(f32[3,8,4,10,1]{4,1,3,2,0:T(8,128)S(1)} %get-tuple-element.72), channel_id=1, source_target_pairs={{0,1},{1,2},{2,3},{3,4},{4,5},{5,6},{6,7},{8,9},{9,10},{10,11},{11... | collective-permute-start | bytes 11528 | tf_op jit(solution)/shard_map/ppermute | solution.py:16
  112.3 14.4 %collective-permute-start.17 = (f32[3,8,4,10,1]{4,1,3,2,0:T(8,128)S(1)}, f32[3,8,4,10,1]{4,1,3,2,0:T(8,128)S(1)}, u32[]{:S(2)}, u32[]{:S(2)}) collective-permute-start(f32[3,8,4,10,1]{4,1,3,2,0:T(8,128)S(1)} %get-tuple-element.73), channel_id=1, source_target_pairs={{1,0},{2,1},{3,2},{4,3},{5,4},{6,5},{7,6},{9,8},{10,9},{11,10},{12... | collective-permute-start | bytes 11528 | tf_op jit(solution)/shard_map/ppermute | solution.py:19
  127.9 4.8 collective-permute-start.18
  130.9 6.0 collective-permute-start.19
  136.8 7.2 %collective-permute-start.20 = (f32[3,8,4,1,128]{4,1,3,2,0:T(8,128)S(1)}, f32[3,8,4,1,128]{4,1,3,2,0:T(8,128)S(1)}, u32[]{:S(2)}, u32[]{:S(2)}) collective-permute-start(f32[3,8,4,1,128]{4,1,3,2,0:T(8,128)S(1)} %get-tuple-element.78), channel_id=1, source_target_pairs={{0,8},{8,16},{16,24},{24,32},{32,40},{40,48},{48,56},{1,9},{9,17},... | collective-permute-start | bytes 147464 | tf_op jit(solution)/shard_map/ppermute | solution.py:16
  142.2 5.4 collective-permute-start.21
  147.8 12.9 %collective-permute-start.22 = (f32[3,8,4,10,1]{4,1,3,2,0:T(8,128)S(1)}, f32[3,8,4,10,1]{4,1,3,2,0:T(8,128)S(1)}, u32[]{:S(2)}, u32[]{:S(2)}) collective-permute-start(f32[3,8,4,10,1]{4,1,3,2,0:T(8,128)S(1)} %get-tuple-element.70), channel_id=1, source_target_pairs={{0,1},{1,2},{2,3},{3,4},{4,5},{5,6},{6,7},{8,9},{9,10},{10,11},{11... | collective-permute-start | bytes 11528 | tf_op jit(solution)/shard_map/ppermute | solution.py:16
  151.5 13.3 %collective-permute-start.23 = (f32[3,8,4,10,1]{4,1,3,2,0:T(8,128)S(1)}, f32[3,8,4,10,1]{4,1,3,2,0:T(8,128)S(1)}, u32[]{:S(2)}, u32[]{:S(2)}) collective-permute-start(f32[3,8,4,10,1]{4,1,3,2,0:T(8,128)S(1)} %get-tuple-element.71), channel_id=1, source_target_pairs={{1,0},{2,1},{3,2},{4,3},{5,4},{6,5},{7,6},{9,8},{10,9},{11,10},{12... | collective-permute-start | bytes 11528 | tf_op jit(solution)/shard_map/ppermute | solution.py:19
  166.0 3.8 collective-permute-start.24
  167.9 6.0 collective-permute-start.25
  173.9 7.0 collective-permute-start.26
  178.7 5.4 collective-permute-start.27
  184.3 13.8 %collective-permute-start.28 = (f32[3,8,4,10,1]{4,1,3,2,0:T(8,128)S(1)}, f32[3,8,4,10,1]{4,1,3,2,0:T(8,128)S(1)}, u32[]{:S(2)}, u32[]{:S(2)}) collective-permute-start(f32[3,8,4,10,1]{4,1,3,2,0:T(8,128)S(1)} %get-tuple-element.68), channel_id=1, source_target_pairs={{0,1},{1,2},{2,3},{3,4},{4,5},{5,6},{6,7},{8,9},{9,10},{10,11},{11... | collective-permute-start | bytes 11528 | tf_op jit(solution)/shard_map/ppermute | solution.py:16
  189.0 13.3 %collective-permute-start.29 = (f32[3,8,4,10,1]{4,1,3,2,0:T(8,128)S(1)}, f32[3,8,4,10,1]{4,1,3,2,0:T(8,128)S(1)}, u32[]{:S(2)}, u32[]{:S(2)}) collective-permute-start(f32[3,8,4,10,1]{4,1,3,2,0:T(8,128)S(1)} %get-tuple-element.69), channel_id=1, source_target_pairs={{1,0},{2,1},{3,2},{4,3},{5,4},{6,5},{7,6},{9,8},{10,9},{11,10},{12... | collective-permute-start | bytes 11528 | tf_op jit(solution)/shard_map/ppermute | solution.py:19
  (3 other events, 7.8 us)
